TPU v7x, 32 devices: a whole 2x2x4 slice. The times are simulated.
32 devices in a mesh: gx: 4 (over z), gy: 2 (over y), gz: 4 (over x, core).
Axes of the slice: x: 2, y: 2, z: 4, core: 2. Of those that a mesh axis runs over, the one named last changes fastest.
Arguments:
- displ: float32 [3, 4, 2, 4, 9945], P(None, 'gx', 'gy', 'gz'), may hold values from -6 to 6
- veloc: float32 [3, 4, 2, 4, 9945], P(None, 'gx', 'gy', 'gz'), may hold values from -6 to 6
- accel: float32 [3, 4, 2, 4, 9945], P(None, 'gx', 'gy', 'gz'), may hold values from -12 to 12
- node_index: int32 [4, 2, 4, 125, 128], P('gx', 'gy', 'gz'), may hold values from 0 to 9944, as said below
- inv_map: float32 [4, 2, 4, 9, 125, 128], P('gx', 'gy', 'gz'), may hold values from -1 to 2, as said below
- jac_weight: float32 [4, 2, 4, 125, 128], P('gx', 'gy', 'gz'), may hold values from 0.05 to 0.5
- lame_first: float32 [4, 2, 4, 125, 128], P('gx', 'gy', 'gz'), may hold values from 0.02 to 0.1
- shear_mod: float32 [4, 2, 4, 125, 128], P('gx', 'gy', 'gz'), may hold values from 0.02 to 0.1
- density: float32 [4, 2, 4, 125, 128], P('gx', 'gy', 'gz'), may hold values from 1 to 3
Outputs:
- displ_out: float32 [3, 4, 2, 4, 9945], P(None, 'gx', 'gy', 'gz')
- veloc_out: float32 [3, 4, 2, 4, 9945], P(None, 'gx', 'gy', 'gz')
- accel_out: float32 [3, 4, 2, 4, 9945], P(None, 'gx', 'gy', 'gz')
Inputs may be any that keep to these rules, and one draw needn't show every extreme that they name: `node_index`: on each device the element slots hold the elements of a brick of 4 x 16 x 2 elements in a drawn order, each once; element (ex, ey, ez) has its point (a, b, c) at node ((4 ex + a) * 65 + 4 ey + b) * 9 + 4 ez + c. `inv_map`: the entries with l equal to j are positive.
All inputs are finite; a program needn't handle non-finite values.
Results may differ from a plain program's by a relative error of at most 0.00024.
Values sent between devices are 32-bit elements; how exact they have to be, the bound alone decides.
A program may use at most 64 MiB of HBM per device.

v0:
```python
import jax
import jax.numpy as jnp
import numpy as np
from jax import lax
from jax.sharding import PartitionSpec as P

EX = 4
EY = 16
EZ = 2


time_step = 0.1


def with_halo(block, sides, width):
    for axis, dim in sides:
        count = lax.axis_size(axis)
        forward = [(i, i + 1) for i in range(count - 1)]
        backward = [(target, source) for source, target in forward]
        low = lax.ppermute(
            lax.slice_in_dim(block, block.shape[dim] - width, None, axis=dim), axis, forward
        )
        high = lax.ppermute(lax.slice_in_dim(block, 0, width, axis=dim), axis, backward)
        block = jnp.concatenate([low, block, high], axis=dim)
    return block


def derivative_table():
    points = np.array([-1.0, -np.sqrt(3.0 / 7.0), 0.0, np.sqrt(3.0 / 7.0), 1.0])
    points_count = points.shape[0]
    weights = np.array(
        [
            1.0
            / np.prod(
                [points[source] - points[other] for other in range(points_count) if other != source]
            )
            for source in range(points_count)
        ]
    )
    deriv_table = np.zeros((points_count, points_count))
    for target in range(points_count):
        for source in range(points_count):
            if target != source:
                deriv_table[target, source] = (
                    weights[source] / weights[target] / (points[target] - points[source])
                )
        deriv_table[target, target] = -np.sum(deriv_table[target])
    return deriv_table


def split_points(grid, dim, count):
    pieces = [
        lax.slice_in_dim(grid, offset, offset + 4 * (count - 1) + 1, stride=4, axis=dim)
        for offset in range(5)
    ]
    return jnp.stack(pieces, axis=dim)


def element_view(grid):
    viewed = split_points(grid, 1, EX)
    viewed = split_points(viewed, 3, EY)
    viewed = split_points(viewed, 5, EZ)
    viewed = jnp.transpose(viewed, (0, 1, 3, 5, 2, 4, 6))
    return viewed.reshape(grid.shape[0], 125, EX * EY * EZ)


def fold_points(terms, axis):
    count = terms.shape[axis + 1]
    lead = lax.slice_in_dim(terms, 0, 4, axis=axis)
    lead = jnp.moveaxis(lead, axis, axis + 1)
    shape = lead.shape[:axis] + (4 * count,) + lead.shape[axis + 2 :]
    lead = lead.reshape(shape)
    widths = [(0, 0)] * len(shape)
    widths[axis] = (0, 1)
    lead = jnp.pad(lead, widths)
    tail = lax.slice_in_dim(terms, 4, 5, axis=axis)
    blank_shape = list(tail.shape)
    blank_shape[axis] = 3
    tail = jnp.concatenate([tail, jnp.zeros(tuple(blank_shape), terms.dtype)], axis=axis)
    tail = jnp.moveaxis(tail, axis, axis + 1).reshape(shape)
    widths[axis] = (4, 0)
    tail = lax.slice_in_dim(jnp.pad(tail, widths), 0, 4 * count + 1, axis=axis)
    return lead + tail


def fold_elements(terms):
    components = terms.shape[0]
    grid = terms.reshape(components, 5, 5, 5, EX, EY, EZ)
    grid = jnp.transpose(grid, (0, 1, 4, 2, 5, 3, 6))
    grid = fold_points(grid, 1)
    grid = fold_points(grid, 2)
    grid = fold_points(grid, 3)
    return grid.reshape(components, (4 * EX + 1) * (4 * EY + 1) * (4 * EZ + 1))


def element_terms(local, mapping, jac_weight, lame_first, shear_mod, deriv):
    highest = lax.Precision.HIGHEST
    elements = local.shape[2]
    local = local.reshape(3, 5, 5, 5, elements)
    grad_a = jnp.einsum("ap,cpbke->cabke", deriv, local, precision=highest).reshape(
        3, 125, elements
    )
    grad_b = jnp.einsum("bp,capke->cabke", deriv, local, precision=highest).reshape(
        3, 125, elements
    )
    grad_c = jnp.einsum("kp,cabpe->cabke", deriv, local, precision=highest).reshape(
        3, 125, elements
    )
    mapping = mapping.reshape(3, 3, 125, elements)
    strain_grad = (
        grad_a[:, None] * mapping[0][None]
        + grad_b[:, None] * mapping[1][None]
        + grad_c[:, None] * mapping[2][None]
    )
    divergence = strain_grad[0, 0] + strain_grad[1, 1] + strain_grad[2, 2]
    identity = jnp.eye(3, dtype=jnp.float32)[:, :, None, None]
    stress = (
        shear_mod * (strain_grad + jnp.swapaxes(strain_grad, 0, 1))
        + lame_first * divergence * identity
    )
    flux = (
        stress[:, 0][:, None] * mapping[:, 0][None]
        + stress[:, 1][:, None] * mapping[:, 1][None]
        + stress[:, 2][:, None] * mapping[:, 2][None]
    )
    flux = (jac_weight * flux).reshape(3, 3, 5, 5, 5, elements)
    terms = jnp.einsum("pa,cpbke->cabke", deriv, flux[:, 0], precision=highest)
    terms = terms + jnp.einsum("pb,capke->cabke", deriv, flux[:, 1], precision=highest)
    terms = terms + jnp.einsum("pk,cabpe->cabke", deriv, flux[:, 2], precision=highest)
    return -terms.reshape(3, 125, elements)


def fold_rim(padded, dim):
    length = padded.shape[dim] - 2
    lower = lax.slice_in_dim(padded, 0, 1, axis=dim)
    upper = lax.slice_in_dim(padded, length + 1, length + 2, axis=dim)
    inner = lax.slice_in_dim(padded, 1, length + 1, axis=dim)
    first = lax.slice_in_dim(inner, 0, 1, axis=dim) + lower
    last = lax.slice_in_dim(inner, length - 1, length, axis=dim) + upper
    middle = lax.slice_in_dim(inner, 1, length - 1, axis=dim)
    return jnp.concatenate([first, middle, last], axis=dim)


def assemble(field):
    node_x = 4 * EX + 1
    node_y = 4 * EY + 1
    node_z = 4 * EZ + 1
    components = field.shape[0]
    node_grid = field.reshape(components, node_x, node_y, node_z)
    node_grid = fold_rim(with_halo(node_grid, (("gx", 1),), 1), 1)
    node_grid = fold_rim(with_halo(node_grid, (("gy", 2),), 1), 2)
    node_grid = fold_rim(with_halo(node_grid, (("gz", 3),), 1), 3)
    return node_grid.reshape(components, node_x * node_y * node_z)


def body(displ, veloc, accel, node_index, inv_map, jac_weight, lame_first, shear_mod, density):
    nodes = displ.shape[4]
    elements = node_index.shape[4]
    node_x = 4 * EX + 1
    node_y = 4 * EY + 1
    node_z = 4 * EZ + 1
    deriv = jnp.asarray(derivative_table(), jnp.float32)
    position = displ.reshape(3, nodes)
    speed = veloc.reshape(3, nodes)
    acceleration = accel.reshape(3, nodes)
    corner = node_index.reshape(125, elements)[0]
    elem_x = corner // (node_y * node_z) // 4
    elem_y = corner // node_z % node_y // 4
    elem_z = corner % node_z // 4
    brick_slot = (elem_x * EY + elem_y) * EZ + elem_z
    slot_of_brick = (
        jnp.zeros((elements,), jnp.int32).at[brick_slot].set(jnp.arange(elements, dtype=jnp.int32))
    )
    mapping = inv_map.reshape(9, 125, elements)[:, :, slot_of_brick]
    weight = jac_weight.reshape(125, elements)[:, slot_of_brick]
    lame = lame_first.reshape(125, elements)[:, slot_of_brick]
    shear = shear_mod.reshape(125, elements)[:, slot_of_brick]
    dens = density.reshape(125, elements)[:, slot_of_brick]
    mass_local = fold_elements((dens * weight)[None])
    mass = assemble(mass_local)[0]
    half_step = 0.5 * time_step
    half_square = 0.5 * time_step * time_step
    position = position + time_step * speed + half_square * acceleration
    speed = speed + half_step * acceleration
    local = element_view(position.reshape(3, node_x, node_y, node_z))
    force = fold_elements(element_terms(local, mapping, weight, lame, shear, deriv))
    force = assemble(force)
    acceleration = force / mass[None]
    speed = speed + half_step * acceleration
    shape = (3, 1, 1, 1, nodes)
    return (position.reshape(shape), speed.reshape(shape), acceleration.reshape(shape))


def solution(mesh):
    placed = (
        P(None, "gx", "gy", "gz", None),
        P(None, "gx", "gy", "gz", None),
        P(None, "gx", "gy", "gz", None),
        P("gx", "gy", "gz", None, None),
        P("gx", "gy", "gz", None, None, None),
        P("gx", "gy", "gz", None, None),
        P("gx", "gy", "gz", None, None),
        P("gx", "gy", "gz", None, None),
        P("gx", "gy", "gz", None, None),
    )
    return jax.shard_map(
        body,
        mesh=mesh,
        in_specs=placed,
        out_specs=(
            P(None, "gx", "gy", "gz", None),
            P(None, "gx", "gy", "gz", None),
            P(None, "gx", "gy", "gz", None),
        ),
        check_vma=False,
    )
```

profile of v0, /device:TPU:1, one launch (start us, length us, event | category | flops | bytes accessed | tf_op | source)
XLA Modules:
  0.0 154.8 jit_solution(11879986830194041598)
XLA Ops:
  0.6 0.7 fusion.19
  1.3 1.0 scatter_custom_fusion
  2.3 0.9 copy.172
  3.3 0.9 copy.231
  4.2 0.7 gather_fusion
  4.9 0.6 gather_fusion.4
  5.5 0.5 mul.282
  6.1 1.6 %slice_bitcast_fusion.1 = f32[1,4,4,5,16,5,2]{5,3,2,6,4,1,0:T(8,128)} fusion(f32[1,5,4,5,16,5,2]{5,3,1,6,4,2,0:T(8,128)S(1)} %bitcast.178), kind=kLoop, calls=%fused_computation.8 | loop fusion | bytes 102400 | tf_op jit(solution)/shard_map/transpose | solution.py:70
  7.7 2.8 %copy.232 = f32[1,4,4,5,16,5,2]{4,2,1,6,5,3,0:T(4,128)S(1)} copy(f32[1,4,4,5,16,5,2]{5,3,2,6,4,1,0:T(8,128)} %slice_bitcast_fusion.1) | data formatting | bytes 102400 | tf_op jit(solution)/shard_map/transpose | solution.py:70
  10.8 1.4 copy.233
  13.6 4.0 %collective-permute-start.6 = (f32[1,1,65,9]{2,3,1,0:T(8,128)S(1)}, f32[1,1,65,9]{2,3,1,0:T(8,128)S(1)}, u32[]{:S(2)}, u32[]{:S(2)}) collective-permute-start(f32[1,1,65,9]{2,3,1,0:T(8,128)S(1)} %get-tuple-element.50), channel_id=1, source_target_pairs={{0,8},{8,16},{16,24},{1,9},{9,17},{17,25},{2,10},{10,18},{18,26},{... | collective-permute-start | bytes 7028 | tf_op jit(solution)/shard_map/ppermute | solution.py:20
  17.6 1.3 collective-permute-start.7
  19.0 1.0 copy.190
  20.0 0.8 gather_fusion.2
  21.1 1.0 fusion.25
  22.1 1.0 fusion.24
  23.1 1.0 add.262
  24.1 1.1 slice_bitcast_fusion.5
  25.2 1.2 copy.180
  26.4 1.2 copy.179
  27.6 1.2 copy.178
  29.4 2.8 %slice.227 = f32[3,5,4,16,9]{3,2,4,1,0:T(4,128)S(1)} slice(f32[3,5,4,65,9]{3,2,4,1,0:T(4,128)S(1)} %constant_dynamic-update-slice_fusion), slice={[0:3:1], [0:5:1], [0:4:1], [4:65:4], [0:9:1]} | slice | bytes 69120 | tf_op jit(solution)/shard_map/slice | solution.py:53
  32.2 2.8 %slice.226 = f32[3,5,4,16,9]{3,2,4,1,0:T(4,128)S(1)} slice(f32[3,5,4,65,9]{3,2,4,1,0:T(4,128)S(1)} %constant_dynamic-update-slice_fusion), slice={[0:3:1], [0:5:1], [0:4:1], [3:64:4], [0:9:1]} | slice | bytes 69120 | tf_op jit(solution)/shard_map/slice | solution.py:53
  35.0 2.8 %slice.225 = f32[3,5,4,16,9]{3,2,4,1,0:T(4,128)S(1)} slice(f32[3,5,4,65,9]{3,2,4,1,0:T(4,128)S(1)} %constant_dynamic-update-slice_fusion), slice={[0:3:1], [0:5:1], [0:4:1], [2:63:4], [0:9:1]} | slice | bytes 69120 | tf_op jit(solution)/shard_map/slice | solution.py:53
  37.7 2.8 %slice.224 = f32[3,5,4,16,9]{3,2,4,1,0:T(4,128)S(1)} slice(f32[3,5,4,65,9]{3,2,4,1,0:T(4,128)S(1)} %constant_dynamic-update-slice_fusion), slice={[0:3:1], [0:5:1], [0:4:1], [1:62:4], [0:9:1]} | slice | bytes 69120 | tf_op jit(solution)/shard_map/slice | solution.py:53
  40.5 2.7 %slice.223 = f32[3,5,4,16,9]{3,2,4,1,0:T(4,128)S(1)} slice(f32[3,5,4,65,9]{3,2,4,1,0:T(4,128)S(1)} %constant_dynamic-update-slice_fusion), slice={[0:3:1], [0:5:1], [0:4:1], [0:61:4], [0:9:1]} | slice | bytes 69120 | tf_op jit(solution)/shard_map/slice | solution.py:53
  43.8 6.9 %copy.186 = f32[3,5,5,5,4,16,2]{3,6,5,4,2,1,0:T(2,128)} copy(f32[3,5,5,5,4,16,2]{5,4,6,1,0,2,3:T(4,128)S(1)} %bitcast.191) | data formatting | bytes 384000 | tf_op jit(solution)/shard_map/transpose | solution.py:63
  50.8 4.7 %copy.192 = f32[3,5,5,5,128]{4,2,3,1,0:T(8,128)S(1)} copy(f32[3,5,5,5,128]{3,4,2,1,0:T(8,128)} %bitcast.172) | data formatting | bytes 384000 | tf_op jit(solution)/shard_map/reshape;reshape | solution.py:99
  55.5 4.9 %copy.187 = f32[3,5,5,5,128]{4,1,3,2,0:T(8,128)S(1)} copy(f32[3,5,5,5,128]{3,4,2,1,0:T(8,128)} %bitcast.173) | data formatting | bytes 384000 | tf_op jit(solution)/shard_map/reshape;reshape | solution.py:99
  60.6 0.7 gather_fusion.3
  61.4 0.6 gather_fusion.1
  62.4 0.7 copy-done
  63.3 6.8 %convolution_bitcast_fusion = f32[3,5,5,5,128]{4,3,2,1,0:T(8,128)S(1)} fusion(f32[3,5,5,5,128]{3,4,2,1,0:T(8,128)} %bitcast.174, f32[5,5,1,1,1]{1,0,4,3,2:T(8,128)S(1)} %copy-done.10), kind=kOutput, calls=%fused_computation.13 | convolution fusion | flops 2880000 | bytes 384100 | tf_op jit(solution)/shard_map/kp,cabpe->cabke/dot_general | solution.py:106
  70.2 0.4 convolution_bitcast_fusion.3
  70.8 0.4 convolution_bitcast_fusion.2
  72.9 0.5 fusion.8
  73.4 0.5 fusion.6
  73.8 0.5 fusion.2
  74.4 3.2 %copy.223 = f32[3,5,5,5,128]{3,4,2,1,0:T(8,128)} copy(f32[3,5,5,5,128]{4,1,3,2,0:T(8,128)S(1)} %fusion.2) | data formatting | bytes 384000 | tf_op jit(solution)/shard_map/neg | solution.py:130
  77.6 1.3 slice.310
  78.9 7.2 %slice_bitcast_fusion = f32[3,4,4,5,16,5,2]{5,6,4,1,3,2,0:T(2,128)} fusion(f32[3,5,4,5,16,5,2]{5,6,4,2,3,1,0:T(2,128)} %bitcast.176), kind=kLoop, calls=%fused_computation.6 | loop fusion | bytes 307200 | tf_op jit(solution)/shard_map/transpose | solution.py:70
  86.1 5.8 %copy.224 = f32[3,4,4,5,16,5,2]{4,2,1,6,5,3,0:T(4,128)S(1)} copy(f32[3,4,4,5,16,5,2]{5,6,4,1,3,2,0:T(2,128)} %slice_bitcast_fusion) | data formatting | bytes 307200 | tf_op jit(solution)/shard_map/transpose | solution.py:70
  91.9 3.9 %pad_bitcast_fusion = f32[3,4,4,5,16,5,2]{5,6,4,1,3,2,0:T(2,128)} fusion(f32[3,1,4,5,16,5,2]{5,6,4,2,3,1,0:T(2,128)S(1)} %slice.310), kind=kLoop, calls=%fused_computation.7 | loop fusion | bytes 192000 | tf_op jit(solution)/shard_map/transpose | solution.py:80
  95.8 5.8 %copy.225 = f32[3,4,4,5,16,5,2]{4,2,1,6,5,3,0:T(4,128)S(1)} copy(f32[3,4,4,5,16,5,2]{5,6,4,1,3,2,0:T(2,128)} %pad_bitcast_fusion) | data formatting | bytes 307200 | tf_op jit(solution)/shard_map/transpose | solution.py:80
  102.2 1.0 copy.226
  103.3 1.0 copy.227
  106.1 3.2 %collective-permute-start.8 = (f32[1,17,1,9]{2,3,1,0:T(8,128)S(1)}, f32[1,17,1,9]{2,3,1,0:T(8,128)S(1)}, u32[]{:S(2)}, u32[]{:S(2)}) collective-permute-start(f32[1,17,1,9]{2,3,1,0:T(8,128)S(1)} %get-tuple-element.46), channel_id=1, source_target_pairs={{0,4},{1,5},{2,6},{3,7},{8,12},{9,13},{10,14},{11,15},{16,20},{17,... | collective-permute-start | bytes 1844 | tf_op jit(solution)/shard_map/ppermute | solution.py:20
  109.3 1.3 collective-permute-start.9
  110.6 4.0 %collective-permute-start = (f32[3,1,65,9]{2,3,1,0:T(8,128)S(1)}, f32[3,1,65,9]{2,3,1,0:T(8,128)S(1)}, u32[]{:S(2)}, u32[]{:S(2)}) collective-permute-start(f32[3,1,65,9]{2,3,1,0:T(8,128)S(1)} %get-tuple-element.42), channel_id=1, source_target_pairs={{0,8},{8,16},{16,24},{1,9},{9,17},{17,25},{2,10},{10,18},{18,26},{... | collective-permute-start | bytes 21068 | tf_op jit(solution)/shard_map/ppermute | solution.py:20
  114.6 1.3 collective-permute-start.1
  116.1 3.0 %collective-permute-done.1 = f32[3,1,65,9]{2,3,1,0:T(8,128)S(1)} collective-permute-done((f32[3,1,65,9]{2,3,1,0:T(8,128)S(1)}, f32[3,1,65,9]{2,3,1,0:T(8,128)S(1)}, u32[]{:S(2)}, u32[]{:S(2)}) %collective-permute-start.1) | collective-permute-done | bytes 7052 | tf_op jit(solution)/shard_map/ppermute | solution.py:23
  119.4 4.0 %collective-permute-start.2 = (f32[3,17,1,9]{2,3,1,0:T(8,128)S(1)}, f32[3,17,1,9]{2,3,1,0:T(8,128)S(1)}, u32[]{:S(2)}, u32[]{:S(2)}) collective-permute-start(f32[3,17,1,9]{2,3,1,0:T(8,128)S(1)} %get-tuple-element.38), channel_id=1, source_target_pairs={{0,4},{1,5},{2,6},{3,7},{8,12},{9,13},{10,14},{11,15},{16,20},{17,... | collective-permute-start | bytes 5516 | tf_op jit(solution)/shard_map/ppermute | solution.py:20
  123.4 1.3 collective-permute-start.3
  124.8 6.5 %collective-permute-start.10 = (f32[1,17,65,1]{2,3,1,0:T(1,128)S(1)}, f32[1,17,65,1]{2,3,1,0:T(1,128)S(1)}, u32[]{:S(2)}, u32[]{:S(2)}) collective-permute-start(f32[1,17,65,1]{2,3,1,0:T(1,128)S(1)} %pad_maximum_fusion.4), channel_id=1, source_target_pairs={{0,1},{1,2},{2,3},{4,5},{5,6},{6,7},{8,9},{9,10},{10,11},{12,13},{... | collective-permute-start | bytes 13268 | tf_op jit(solution)/shard_map/ppermute | solution.py:20
  131.5 1.5 collective-permute-done.3
  133.4 7.4 %collective-permute-start.4 = (f32[3,17,65,1]{2,3,1,0:T(1,128)S(1)}, f32[3,17,65,1]{2,3,1,0:T(1,128)S(1)}, u32[]{:S(2)}, u32[]{:S(2)}) collective-permute-start(f32[3,17,65,1]{2,3,1,0:T(1,128)S(1)} %pad_maximum_fusion.2), channel_id=1, source_target_pairs={{0,1},{1,2},{2,3},{4,5},{5,6},{6,7},{8,9},{9,10},{10,11},{12,13},{... | collective-permute-start | bytes 39788 | tf_op jit(solution)/shard_map/ppermute | solution.py:20
  140.9 1.9 %collective-permute-start.11 = (f32[1,17,65,1]{2,3,1,0:T(1,128)S(1)}, f32[1,17,65,1]{2,3,1,0:T(1,128)S(1)}, u32[]{:S(2)}, u32[]{:S(2)}) collective-permute-start(f32[1,17,65,1]{2,3,1,0:T(1,128)S(1)} %get-tuple-element.15), channel_id=1, source_target_pairs={{1,0},{2,1},{3,2},{5,4},{6,5},{7,6},{9,8},{10,9},{11,10},{13,12},{... | collective-permute-start | bytes 13268 | tf_op jit(solution)/shard_map/ppermute | solution.py:23
  142.8 3.0 %collective-permute-done.11 = f32[1,17,65,1]{2,3,1,0:T(1,128)S(1)} collective-permute-done((f32[1,17,65,1]{2,3,1,0:T(1,128)S(1)}, f32[1,17,65,1]{2,3,1,0:T(1,128)S(1)}, u32[]{:S(2)}, u32[]{:S(2)}) %collective-permute-start.11) | collective-permute-done | bytes 4452 | tf_op jit(solution)/shard_map/ppermute | solution.py:23
  146.1 1.9 %collective-permute-start.5 = (f32[3,17,65,1]{2,3,1,0:T(1,128)S(1)}, f32[3,17,65,1]{2,3,1,0:T(1,128)S(1)}, u32[]{:S(2)}, u32[]{:S(2)}) collective-permute-start(f32[3,17,65,1]{2,3,1,0:T(1,128)S(1)} %get-tuple-element.17), channel_id=1, source_target_pairs={{1,0},{2,1},{3,2},{5,4},{6,5},{7,6},{9,8},{10,9},{11,10},{13,12},{... | collective-permute-start | bytes 39788 | tf_op jit(solution)/shard_map/ppermute | solution.py:23
  148.8 2.4 %collective-permute-done.5 = f32[3,17,65,1]{2,3,1,0:T(1,128)S(1)} collective-permute-done((f32[3,17,65,1]{2,3,1,0:T(1,128)S(1)}, f32[3,17,65,1]{2,3,1,0:T(1,128)S(1)}, u32[]{:S(2)}, u32[]{:S(2)}) %collective-permute-start.5) | collective-permute-done | bytes 13292 | tf_op jit(solution)/shard_map/ppermute | solution.py:23
  151.4 0.7 copy.230
  152.2 0.7 reshape.499
  153.3 0.8 copy.239
  154.0 0.8 copy.240
  (148 shorter events, 10.9 us)
Async XLA Ops:
  13.1 5.9 %copy-start.5 = (f32[1,1,1,9,125,128]{5,2,4,3,1,0:T(1,128)S(1)}, f32[1,1,1,9,125,128]{5,2,4,3,1,0:T(1,128)}, u32[]{:S(2)}) copy-start(f32[1,1,1,9,125,128]{5,2,4,3,1,0:T(1,128)} %param.14) | copy-start | bytes 1728004
  13.6 5.3 %copy-start.3 = (f32[1,17,65,9]{2,3,1,0:T(8,128)}, f32[1,17,65,9]{2,3,1,0:T(8,128)S(1)}, u32[]{:S(2)}) copy-start(f32[1,17,65,9]{2,3,1,0:T(8,128)S(1)} %slice_add_fusion.5) | copy-start | bytes 119344
  13.6 91.9 %collective-permute-start.6 = (f32[1,1,65,9]{2,3,1,0:T(8,128)S(1)}, f32[1,1,65,9]{2,3,1,0:T(8,128)S(1)}, u32[]{:S(2)}, u32[]{:S(2)}) collective-permute-start(f32[1,1,65,9]{2,3,1,0:T(8,128)S(1)} %get-tuple-element.50), channel_id=1, source_target_pairs={{0,8},{8,16},{16,24},{1,9},{9,17},{17,25},{2,10},{10,18},{18,26},{... | collective-permute-start | bytes 7028 | tf_op jit(solution)/shard_map/ppermute | solution.py:20
  17.6 87.9 %collective-permute-start.7 = (f32[1,1,65,9]{2,3,1,0:T(8,128)S(1)}, f32[1,1,65,9]{2,3,1,0:T(8,128)S(1)}, u32[]{:S(2)}, u32[]{:S(2)}) collective-permute-start(f32[1,1,65,9]{2,3,1,0:T(8,128)S(1)} %get-tuple-element.51), channel_id=1, source_target_pairs={{8,0},{16,8},{24,16},{9,1},{17,9},{25,17},{10,2},{18,10},{26,18},{... | collective-permute-start | bytes 7028 | tf_op jit(solution)/shard_map/ppermute | solution.py:23
  20.8 1.3 copy-start.6
  20.8 1.3 copy-start.8
  20.8 1.3 copy-start.11
  55.5 5.1 %copy-start.12 = (f32[1,1,1,125,128]{4,2,3,1,0:T(1,128)S(1)}, f32[1,1,1,125,128]{4,2,3,1,0:T(1,128)}, u32[]{:S(2)}) copy-start(f32[1,1,1,125,128]{4,2,3,1,0:T(1,128)} %param.16) | copy-start | bytes 192004
  55.5 5.8 %copy-start.13 = (f32[1,1,1,125,128]{4,2,3,1,0:T(1,128)S(1)}, f32[1,1,1,125,128]{4,2,3,1,0:T(1,128)}, u32[]{:S(2)}) copy-start(f32[1,1,1,125,128]{4,2,3,1,0:T(1,128)} %param.17) | copy-start | bytes 192004
  60.4 1.7 %copy-start.2 = (f32[3,125,128]{1,0,2:T(4,128)S(1)}, f32[3,125,128]{1,0,2:T(4,128)}, u32[]{:S(2)}) copy-start(f32[3,125,128]{1,0,2:T(4,128)} %get-tuple-element.25) | copy-start | bytes 576004
  61.4 1.0 copy-start.1
  62.1 1.0 copy-start
  62.4 0.9 copy-start.10
  105.0 0.9 copy-start.4
  105.0 1.0 slice-start
  106.1 9.9 %collective-permute-start.8 = (f32[1,17,1,9]{2,3,1,0:T(8,128)S(1)}, f32[1,17,1,9]{2,3,1,0:T(8,128)S(1)}, u32[]{:S(2)}, u32[]{:S(2)}) collective-permute-start(f32[1,17,1,9]{2,3,1,0:T(8,128)S(1)} %get-tuple-element.46), channel_id=1, source_target_pairs={{0,4},{1,5},{2,6},{3,7},{8,12},{9,13},{10,14},{11,15},{16,20},{17,... | collective-permute-start | bytes 1844 | tf_op jit(solution)/shard_map/ppermute | solution.py:20
  109.3 6.7 %collective-permute-start.9 = (f32[1,17,1,9]{2,3,1,0:T(8,128)S(1)}, f32[1,17,1,9]{2,3,1,0:T(8,128)S(1)}, u32[]{:S(2)}, u32[]{:S(2)}) collective-permute-start(f32[1,17,1,9]{2,3,1,0:T(8,128)S(1)} %get-tuple-element.47), channel_id=1, source_target_pairs={{4,0},{5,1},{6,2},{7,3},{12,8},{13,9},{14,10},{15,11},{20,16},{21,... | collective-permute-start | bytes 1844 | tf_op jit(solution)/shard_map/ppermute | solution.py:23
  110.6 5.5 %collective-permute-start = (f32[3,1,65,9]{2,3,1,0:T(8,128)S(1)}, f32[3,1,65,9]{2,3,1,0:T(8,128)S(1)}, u32[]{:S(2)}, u32[]{:S(2)}) collective-permute-start(f32[3,1,65,9]{2,3,1,0:T(8,128)S(1)} %get-tuple-element.42), channel_id=1, source_target_pairs={{0,8},{8,16},{16,24},{1,9},{9,17},{17,25},{2,10},{10,18},{18,26},{... | collective-permute-start | bytes 21068 | tf_op jit(solution)/shard_map/ppermute | solution.py:20
  114.6 4.6 %collective-permute-start.1 = (f32[3,1,65,9]{2,3,1,0:T(8,128)S(1)}, f32[3,1,65,9]{2,3,1,0:T(8,128)S(1)}, u32[]{:S(2)}, u32[]{:S(2)}) collective-permute-start(f32[3,1,65,9]{2,3,1,0:T(8,128)S(1)} %get-tuple-element.43), channel_id=1, source_target_pairs={{8,0},{16,8},{24,16},{9,1},{17,9},{25,17},{10,2},{18,10},{26,18},{... | collective-permute-start | bytes 21068 | tf_op jit(solution)/shard_map/ppermute | solution.py:23
  119.4 12.1 %collective-permute-start.2 = (f32[3,17,1,9]{2,3,1,0:T(8,128)S(1)}, f32[3,17,1,9]{2,3,1,0:T(8,128)S(1)}, u32[]{:S(2)}, u32[]{:S(2)}) collective-permute-start(f32[3,17,1,9]{2,3,1,0:T(8,128)S(1)} %get-tuple-element.38), channel_id=1, source_target_pairs={{0,4},{1,5},{2,6},{3,7},{8,12},{9,13},{10,14},{11,15},{16,20},{17,... | collective-permute-start | bytes 5516 | tf_op jit(solution)/shard_map/ppermute | solution.py:20
  123.4 9.6 %collective-permute-start.3 = (f32[3,17,1,9]{2,3,1,0:T(8,128)S(1)}, f32[3,17,1,9]{2,3,1,0:T(8,128)S(1)}, u32[]{:S(2)}, u32[]{:S(2)}) collective-permute-start(f32[3,17,1,9]{2,3,1,0:T(8,128)S(1)} %get-tuple-element.39), channel_id=1, source_target_pairs={{4,0},{5,1},{6,2},{7,3},{12,8},{13,9},{14,10},{15,11},{20,16},{21,... | collective-permute-start | bytes 5516 | tf_op jit(solution)/shard_map/ppermute | solution.py:23
  124.8 15.9 %collective-permute-start.10 = (f32[1,17,65,1]{2,3,1,0:T(1,128)S(1)}, f32[1,17,65,1]{2,3,1,0:T(1,128)S(1)}, u32[]{:S(2)}, u32[]{:S(2)}) collective-permute-start(f32[1,17,65,1]{2,3,1,0:T(1,128)S(1)} %pad_maximum_fusion.4), channel_id=1, source_target_pairs={{0,1},{1,2},{2,3},{4,5},{5,6},{6,7},{8,9},{9,10},{10,11},{12,13},{... | collective-permute-start | bytes 13268 | tf_op jit(solution)/shard_map/ppermute | solution.py:20
  133.4 12.5 %collective-permute-start.4 = (f32[3,17,65,1]{2,3,1,0:T(1,128)S(1)}, f32[3,17,65,1]{2,3,1,0:T(1,128)S(1)}, u32[]{:S(2)}, u32[]{:S(2)}) collective-permute-start(f32[3,17,65,1]{2,3,1,0:T(1,128)S(1)} %pad_maximum_fusion.2), channel_id=1, source_target_pairs={{0,1},{1,2},{2,3},{4,5},{5,6},{6,7},{8,9},{9,10},{10,11},{12,13},{... | collective-permute-start | bytes 39788 | tf_op jit(solution)/shard_map/ppermute | solution.py:20
  140.9 5.0 %collective-permute-start.11 = (f32[1,17,65,1]{2,3,1,0:T(1,128)S(1)}, f32[1,17,65,1]{2,3,1,0:T(1,128)S(1)}, u32[]{:S(2)}, u32[]{:S(2)}) collective-permute-start(f32[1,17,65,1]{2,3,1,0:T(1,128)S(1)} %get-tuple-element.15), channel_id=1, source_target_pairs={{1,0},{2,1},{3,2},{5,4},{6,5},{7,6},{9,8},{10,9},{11,10},{13,12},{... | collective-permute-start | bytes 13268 | tf_op jit(solution)/shard_map/ppermute | solution.py:23
  146.1 5.2 %collective-permute-start.5 = (f32[3,17,65,1]{2,3,1,0:T(1,128)S(1)}, f32[3,17,65,1]{2,3,1,0:T(1,128)S(1)}, u32[]{:S(2)}, u32[]{:S(2)}) collective-permute-start(f32[3,17,65,1]{2,3,1,0:T(1,128)S(1)} %get-tuple-element.17), channel_id=1, source_target_pairs={{1,0},{2,1},{3,2},{5,4},{6,5},{7,6},{9,8},{10,9},{11,10},{13,12},{... | collective-permute-start | bytes 39788 | tf_op jit(solution)/shard_map/ppermute | solution.py:23
  152.2 0.9 copy-start.7
  152.2 1.0 copy-start.9
where the time goes:
time: 156 us; the launch traced here: 155 us
  local copies, waits for them, and re-layouts  91.5 us (59%)
  starting transfers between devices  38 us (24%)
  waiting for transfers between devices  9.99 us (6%)
  matrix products  8.98 us (6%)
  other arithmetic  4.51 us (3%)
  between operations  1.8 us (1%)
    ppermute x6, starting transfers between devices, with_halo(): lax.ppermute(lax.slice_in_dim(block, block.shape[dim] - width, None, axis...  29 us
    transpose x12, local copies, waits for them, and re-layouts, fold_points(): lead = jnp.moveaxis(lead, axis, axis + 1)  19.6 us
    slice x5, local copies, waits for them, and re-layouts, split_points(): lax.slice_in_dim(grid, offset, offset + 4 * (count - 1) + 1, stride=4, ax...  13.8 us
    transpose x12, local copies, waits for them, and re-layouts, fold_points(): tail = jnp.moveaxis(tail, axis, axis + 1).reshape(shape)  13.5 us
    ppermute x6, waiting for transfers between devices, with_halo(): lax.ppermute(lax.slice_in_dim(block, 0, width, axis=dim), axis, backward)  9.97 us
    another operation x2, local copies, waits for them, and re-layouts, element_terms(): local = local.reshape(3, 5, 5, 5, elements)  9.54 us
    ppermute x6, starting transfers between devices, with_halo(): lax.ppermute(lax.slice_in_dim(block, 0, width, axis=dim), axis, backward)  9.01 us
    transpose x1, local copies, waits for them, and re-layouts, element_view(): viewed = jnp.transpose(viewed, (0, 1, 3, 5, 2, 4, 6))  6.94 us
  transfers between devices with their start and end apart: 12, of which 4 were waited for; matrix products, arithmetic and copies ran while one was open for 56% of the time, Pallas kernels for 0%

commit v1 on v0

v1 whole, which is shorter than its diff:
```python
import jax
import jax.numpy as jnp
import numpy as np
from jax import lax
from jax.experimental import pallas as pl
from jax.experimental.pallas import tpu as pltpu
from jax.sharding import PartitionSpec as P

EX = 4
EY = 16
EZ = 2
NX = 4 * EX + 1
NY = 4 * EY + 1
NZ = 4 * EZ + 1
PLANE = NY * NZ
GROUP = 4
GROUPS = EY // GROUP
STEP = 4 * GROUP * NZ
SPAN = 256
WIDE = 640
GROW = 64
SROW = 72
SUB = EZ * GROUP

time_step = 0.1
MESH = pl.DeviceIdType.MESH


def derivative_table():
    points = np.array([-1.0, -np.sqrt(3.0 / 7.0), 0.0, np.sqrt(3.0 / 7.0), 1.0])
    count = points.shape[0]
    weights = np.array(
        [
            1.0 / np.prod([points[s] - points[o] for o in range(count) if o != s])
            for s in range(count)
        ]
    )
    table = np.zeros((count, count))
    for t in range(count):
        for s in range(count):
            if t != s:
                table[t, s] = weights[s] / weights[t] / (points[t] - points[s])
        table[t, t] = -np.sum(table[t])
    return table


def constants():
    table = derivative_table()
    select = np.zeros((25 * SUB, SPAN), np.float32)
    for b in range(5):
        for c in range(5):
            for ez in range(EZ):
                for ey in range(GROUP):
                    row = (b * 5 + c) * SUB + ez * GROUP + ey
                    select[row, (4 * ey + b) * NZ + 4 * ez + c] = 1.0
    eye = np.eye(5)
    parts = [
        np.kron(table, np.kron(eye, eye)),
        np.kron(eye, np.kron(table, eye)),
        np.kron(eye, np.kron(eye, table)),
    ]
    pad = np.zeros((125, 160))
    for a in range(5):
        for q in range(25):
            pad[a * 25 + q, a * 32 + q] = 1.0
    deriv = np.zeros((384, 160), np.float32)
    for l in range(3):
        deriv[l * 128 : l * 128 + 125] = parts[l] @ pad
    spread = np.zeros((160, 128), np.float32)
    spread[:, :125] = pad.T
    return select, deriv, -deriv.T.copy(), spread


def split3(x):
    hi = x.astype(jnp.bfloat16)
    rest = x - hi.astype(jnp.float32)
    mid = rest.astype(jnp.bfloat16)
    low = (rest - mid.astype(jnp.float32)).astype(jnp.bfloat16)
    return (hi, mid, low)


def dots(x, y, dims, split_left):
    total = None
    for piece in split3(x if split_left else y):
        left, right = (piece, y) if split_left else (x, piece)
        out = lax.dot_general(
            left, right, (dims, ((), ())), preferred_element_type=jnp.float32
        )
        total = out if total is None else total + out
    return total


def kernel(
    displ, veloc, accel, node, inv, jac, lame, shear, dens,
    select_ref, deriv_ref, back_ref, spread_ref,
    pos_out, spd_out, acc_out,
    d_s, v_s, a_s, node_s, inv_s, jac_s, lame_s, shear_s, dens_s,
    nf, u_s, fl_s, md_s, zp_s, grid_s, acc_s,
    z_send, z_recv, y_send, y_recv, x_send, x_recv,
    in_sem, out_sem, send_sem, recv_sem,
):
    names = ("gz", "gy", "gx")
    spots = [lax.axis_index(n) for n in names]
    sizes = [lax.axis_size(n) for n in names]
    has_low = [s > 0 for s in spots]
    has_high = [s < n - 1 for s, n in zip(spots, sizes)]
    barrier = pltpu.get_barrier_semaphore()
    for n, s, lo, hi in zip(names, spots, has_low, has_high):

        @pl.when(lo)
        def _():
            pl.semaphore_signal(barrier, inc=1, device_id={n: s - 1}, device_id_type=MESH)

        @pl.when(hi)
        def _():
            pl.semaphore_signal(barrier, inc=1, device_id={n: s + 1}, device_id_type=MESH)

    copies = []
    for k, (src, dst) in enumerate(((displ, d_s), (veloc, v_s), (accel, a_s))):
        for c in range(3):
            copies.append(
                pltpu.make_async_copy(
                    src.at[c], dst.at[pl.ds(c, 1)], in_sem.at[3 * k + c]
                )
            )
    elems = ((node, node_s), (inv, inv_s), (jac, jac_s), (lame, lame_s), (shear, shear_s), (dens, dens_s))
    for k, (src, dst) in enumerate(elems):
        copies.append(pltpu.make_async_copy(ELEM_SRC(src), dst, in_sem.at[9 + k]))
    for cp in copies:
        cp.start()
    nf[...] = jnp.zeros_like(nf)
    u_s[...] = jnp.zeros_like(u_s)
    fl_s[...] = jnp.zeros_like(fl_s)
    md_s[...] = jnp.zeros_like(md_s)
    for cp in copies[:10]:
        cp.wait()

    half = 0.5 * time_step
    pos = d_s[...] + time_step * v_s[...] + (half * time_step) * a_s[...]
    d_s[...] = pos
    v_s[...] = v_s[...] + half * a_s[...]
    pos_copies = [
        pltpu.make_async_copy(d_s.at[pl.ds(c, 1)], pos_out.at[c], out_sem.at[c])
        for c in range(3)
    ]
    for cp in pos_copies:
        cp.start()

    for x in range(NX):
        nf[3 * x : 3 * x + 3, 0:PLANE] = d_s[:, PLANE * x : PLANE * (x + 1)]
    planes = nf[...]
    blocks = [planes[:, :SPAN]] + [
        pltpu.roll(planes, WIDE - STEP * g, 1)[:, :SPAN] for g in range(1, GROUPS)
    ]
    rows = jnp.concatenate(blocks, axis=0)
    select = select_ref[...]
    lifted = dots(select, rows, ((1,), (1,)), False)

    corner = node_s[0:1, :].astype(jnp.float32)
    x0 = jnp.floor((corner + 0.5) * (1.0 / PLANE))
    rem = corner - PLANE * x0
    y0 = jnp.floor((rem + 0.5) * (1.0 / NZ))
    z0 = rem - NZ * y0
    grp = jnp.floor((y0 + 0.5) * (1.0 / (4 * GROUP)))
    low = (y0 - 4 * GROUP * grp) * 0.25 + GROUP * (z0 * 0.25)
    sub = lax.broadcasted_iota(jnp.int32, (SUB, 128), 0).astype(jnp.float32)
    mask = jnp.where(sub == low, 1.0, 0.0)[None]

    iota = lax.broadcasted_iota(jnp.int32, (GROUPS * GROW, 128), 0).astype(jnp.float32)
    goal = grp * GROW + 3.0 * x0
    picks = jnp.concatenate(
        [
            jnp.where(iota == goal + (3.0 * a + c), 1.0, 0.0).astype(jnp.bfloat16)
            for c in range(3)
            for a in range(5)
        ],
        axis=1,
    )
    gathered = dots(lifted, picks, ((1,), (0,)), True)
    for c in range(3):
        for a in range(5):
            j = (c * 5 + a) * 128
            part = gathered[:, j : j + 128].reshape(25, SUB, 128) * mask
            u_s[a * 32 : a * 32 + 25, c * 128 : (c + 1) * 128] = jnp.sum(part, axis=1)

    highest = lax.Precision.HIGHEST
    local = jnp.dot(
        deriv_ref[...], u_s[...], precision=highest, preferred_element_type=jnp.float32
    )
    for cp in copies[10:]:
        cp.wait()
    grads = [
        [local[l * 128 : l * 128 + 125, c * 128 : (c + 1) * 128] for c in range(3)]
        for l in range(3)
    ]
    maps = [[inv_s[INV_ROWS(3 * l + j)] for j in range(3)] for l in range(3)]
    weight = jac_s[...]
    lam = lame_s[...]
    mu = shear_s[...]
    h = [
        [sum(grads[l][c] * maps[l][j] for l in range(3)) for j in range(3)] for c in range(3)
    ]
    div = lam * (h[0][0] + h[1][1] + h[2][2])
    stress = [[None] * 3 for _ in range(3)]
    for c in range(3):
        for j in range(c, 3):
            s = mu * (h[c][j] + h[j][c])
            if c == j:
                s = s + div
            s = s * weight
            stress[c][j] = s
            stress[j][c] = s
    for l in range(3):
        for c in range(3):
            fl_s[l * 128 : l * 128 + 125, c * 128 : (c + 1) * 128] = sum(
                stress[c][j] * maps[l][j] for j in range(3)
            )
    md_s[0:125, :] = dens_s[...] * weight
    terms = jnp.dot(
        back_ref[...], fl_s[...], precision=highest, preferred_element_type=jnp.float32
    )
    heavy = jnp.dot(
        spread_ref[...], md_s[...], precision=highest, preferred_element_type=jnp.float32
    )

    spread_out = []
    puts = []
    iota2 = lax.broadcasted_iota(jnp.int32, (GROUPS * SROW, 128), 0).astype(jnp.float32)
    goal2 = grp * SROW + 4.0 * x0
    for k in range(4):
        for a in range(5):
            part = terms[a * 32 : a * 32 + 25, k * 128 : (k + 1) * 128] if k < 3 else heavy[a * 32 : a * 32 + 25]
            spread_out.append((part[:, None, :] * mask).reshape(25 * SUB, 128))
            puts.append(
                jnp.where(iota2 == goal2 + (4.0 * a + k), 1.0, 0.0).astype(jnp.bfloat16)
            )
    zp_s[...] = dots(
        jnp.concatenate(spread_out, axis=1),
        jnp.concatenate(puts, axis=1),
        ((1,), (1,)),
        True,
    )

    peers = sum(flag.astype(jnp.int32) for flag in has_low + has_high)
    pl.semaphore_wait(barrier, peers)

    def exchange(axis, send, recv):
        name, spot = names[axis], spots[axis]

        def copy(side, peer):
            return pltpu.make_async_remote_copy(
                src_ref=send.at[side],
                dst_ref=recv.at[1 - side],
                send_sem=send_sem.at[2 * axis + side],
                recv_sem=recv_sem.at[2 * axis + 1 - side],
                device_id={name: peer},
                device_id_type=MESH,
            )

        @pl.when(has_low[axis])
        def _():
            copy(0, spot - 1).start()

        @pl.when(has_high[axis])
        def _():
            copy(1, spot + 1).start()

        def finish(side):
            copy(1 - side, spot).wait_recv()

        def drain():
            for side, ok in ((0, has_low[axis]), (1, has_high[axis])):

                @pl.when(ok)
                def _():
                    copy(side, spot).wait_send()

        return finish, drain

    drains = []
    for b in range(5):
        z_send[0, b * 4 : b * 4 + 4] = zp_s[b * 5 * SUB : b * 5 * SUB + GROUP]
        top = (b * 5 + 4) * SUB + (EZ - 1) * GROUP
        z_send[1, b * 4 : b * 4 + 4] = zp_s[top : top + GROUP]
    finish, drain = exchange(0, z_send, z_recv)
    drains.append(drain)

    @pl.when(has_low[0])
    def _():
        finish(0)
        for b in range(5):
            at = b * 5 * SUB
            zp_s[at : at + GROUP] += z_recv[0, b * 4 : b * 4 + 4]

    @pl.when(has_high[0])
    def _():
        finish(1)
        for b in range(5):
            at = (b * 5 + 4) * SUB + (EZ - 1) * GROUP
            zp_s[at : at + GROUP] += z_recv[1, b * 4 : b * 4 + 4]

    flat = dots(zp_s[...], select, ((0,), (0,)), True)
    total = None
    blank = jnp.zeros((SROW, WIDE - SPAN), jnp.float32)
    for g in range(GROUPS):
        piece = jnp.concatenate([flat[g * SROW : (g + 1) * SROW], blank], axis=1)
        if g:
            piece = pltpu.roll(piece, STEP * g, 1)
        total = piece if total is None else total + piece
    grid_s[...] = total

    edge = WIDE - 128
    shift = PLANE - NZ - edge
    lanes = lax.broadcasted_iota(jnp.int32, (SROW, 128), 1)
    y_send[0] = grid_s[:, 0:128]
    y_send[1] = grid_s[:, edge:WIDE]
    finish, drain = exchange(1, y_send, y_recv)
    drains.append(drain)

    @pl.when(has_low[1])
    def _():
        finish(0)
        got = pltpu.roll(y_recv[0], 128 - shift, 1)
        grid_s[:, 0:128] += jnp.where(lanes < NZ, got, 0.0)

    @pl.when(has_high[1])
    def _():
        finish(1)
        got = jnp.where(lanes < NZ, y_recv[1], 0.0)
        grid_s[:, edge:WIDE] += pltpu.roll(got, shift, 1)

    x_send[0] = grid_s[0:8]
    x_send[1] = grid_s[SROW - 8 : SROW]
    finish, drain = exchange(2, x_send, x_recv)
    drains.append(drain)

    @pl.when(has_low[2])
    def _():
        finish(0)
        grid_s[0:4] += x_recv[0, 0:4]

    @pl.when(has_high[2])
    def _():
        finish(1)
        grid_s[SROW - 8 : SROW - 4] += x_recv[1, 0:4]

    for x in range(NX):
        force = grid_s[4 * x : 4 * x + 3, 0:PLANE]
        mass = grid_s[4 * x + 3 : 4 * x + 4, 0:PLANE]
        acc_s[:, PLANE * x : PLANE * (x + 1)] = force / mass
    v_s[...] = v_s[...] + half * acc_s[...]
    last = []
    for k, (src, dst) in enumerate(((v_s, spd_out), (acc_s, acc_out))):
        for c in range(3):
            last.append(
                pltpu.make_async_copy(
                    src.at[pl.ds(c, 1)], dst.at[c], out_sem.at[3 + 3 * k + c]
                )
            )
    for cp in last:
        cp.start()
    for drain in drains:
        drain()
    for cp in pos_copies + last:
        cp.wait()


def ELEM_SRC(ref):
    return ref


def INV_ROWS(k):
    return (k,)


def body(displ, veloc, accel, node_index, inv_map, jac_weight, lame_first, shear_mod, density):
    nodes = displ.shape[4]
    elements = node_index.shape[4]
    select, deriv, back, spread = constants()
    fields = [x.reshape(3, 1, nodes) for x in (displ, veloc, accel)]
    elems = [
        x.reshape(125, elements) for x in (jac_weight, lame_first, shear_mod, density)
    ]
    hbm = pl.BlockSpec(memory_space=pl.ANY)
    vmem = pl.BlockSpec(memory_space=pltpu.VMEM)
    f32 = jnp.float32
    out = jax.ShapeDtypeStruct((3, 1, nodes), f32)
    elem = pltpu.VMEM((125, elements), f32)
    width = GROUPS * SROW
    outs = pl.pallas_call(
        kernel,
        out_shape=(out, out, out),
        in_specs=[hbm] * 9 + [vmem] * 4,
        out_specs=(hbm, hbm, hbm),
        scratch_shapes=[
            pltpu.VMEM((3, nodes), f32),
            pltpu.VMEM((3, nodes), f32),
            pltpu.VMEM((3, nodes), f32),
            pltpu.VMEM((125, elements), jnp.int32),
            pltpu.VMEM((9, 125, elements), f32),
            elem, elem, elem, elem,
            pltpu.VMEM((GROW, WIDE), f32),
            pltpu.VMEM((160, 384), f32),
            pltpu.VMEM((384, 384), f32),
            pltpu.VMEM((128, 128), f32),
            pltpu.VMEM((25 * SUB, width), f32),
            pltpu.VMEM((SROW, WIDE), f32),
            pltpu.VMEM((3, nodes), f32),
            pltpu.VMEM((2, 24, width), f32),
            pltpu.VMEM((2, 24, width), f32),
            pltpu.VMEM((2, SROW, 128), f32),
            pltpu.VMEM((2, SROW, 128), f32),
            pltpu.VMEM((2, 8, WIDE), f32),
            pltpu.VMEM((2, 8, WIDE), f32),
            pltpu.SemaphoreType.DMA((15,)),
            pltpu.SemaphoreType.DMA((9,)),
            pltpu.SemaphoreType.DMA((6,)),
            pltpu.SemaphoreType.DMA((6,)),
        ],
        compiler_params=pltpu.CompilerParams(collective_id=0, has_side_effects=True),
    )(
        *fields,
        node_index.reshape(125, elements),
        inv_map.reshape(9, 125, elements),
        *elems,
        jnp.asarray(select, jnp.bfloat16),
        jnp.asarray(deriv),
        jnp.asarray(back),
        jnp.asarray(spread),
    )
    shape = (3, 1, 1, 1, nodes)
    return tuple(x.reshape(shape) for x in outs)


def solution(mesh):
    field = P(None, "gx", "gy", "gz", None)
    elem = P("gx", "gy", "gz", None, None)
    placed = (field,) * 3 + (elem, P("gx", "gy", "gz", None, None, None)) + (elem,) * 4
    return jax.shard_map(
        body, mesh=mesh, in_specs=placed, out_specs=(field,) * 3, check_vma=False
    )
```

time: 156 us -> 29.1 us (0.19)
  local copies, waits for them, and re-layouts: 91.5 us -> 8.63 us
  starting transfers between devices: 38 us -> 0 us
  Pallas kernels: 0 us -> 19.5 us
  waiting for transfers between devices: 9.99 us -> 0 us
  matrix products: 8.98 us -> 0 us
  other arithmetic: 4.51 us -> 0 us
    transpose x27 -> x0, local copies, waits for them, and re-layouts: 40.1 us -> none  [the longest x12 19.6 us: fold_points(): lead = jnp.moveaxis(lead, axis, axis + 1)]
    ppermute x12 -> x0, starting transfers between devices: 38 us -> none  [the longest x6 29 us: with_halo(): lax.ppermute(lax.slice_in_dim(block, block.shape[dim] - width, None, axis...]
    pallas_call x0 -> x1, Pallas kernels: none -> 19.5 us  [body(): pl.pallas_call(kernel, out_shape=(out, out, out), in_specs=[hbm] * 9 + [v...]
    slice x29 -> x0, local copies, waits for them, and re-layouts: 17.3 us -> none  [the longest x5 13.8 us: split_points(): lax.slice_in_dim(grid, offset, offset + 4 * (count - 1) + 1, stride=4, ax...]
    another operation x11 -> x0, local copies, waits for them, and re-layouts: 14.9 us -> none  [the longest x2 9.54 us: element_terms(): local = local.reshape(3, 5, 5, 5, elements)]
    ppermute x12 -> x0, waiting for transfers between devices: 9.99 us -> none  [the longest x6 9.97 us: with_halo(): lax.ppermute(lax.slice_in_dim(block, 0, width, axis=dim), axis, backward)]
    dot_general x6 -> x0, matrix products: 8.98 us -> none  [the longest x1 6.76 us: element_terms(): jnp.einsum('kp,cabpe->cabke', deriv, local, precision=highest)]
    gather x7 -> x0, local copies, waits for them, and re-layouts: 3.78 us -> none  [the longest x2 1.09 us: body(): mapping = inv_map.reshape(9, 125, elements)[:, :, slot_of_brick]]
  transfers between devices with their start and end apart: 12 -> 0, of which waited for: 4 -> 0; matrix products, arithmetic and copies ran while one was open for 56% -> 0% of each run, Pallas kernels for 0% -> 0%
where the time goes in v1:
time: 29.1 us; the launch traced here: 28.8 us
  Pallas kernels  19.5 us (67%)
  local copies, waits for them, and re-layouts  8.63 us (30%)
  between operations  0.66 us (2%)
    pallas_call x1, Pallas kernels, body(): pl.pallas_call(kernel, out_shape=(out, out, out), in_specs=[hbm] * 9 + [v...  19.5 us
    unnamed x13, local copies, waits for them, and re-layouts  8.63 us

profile of v1, /device:TPU:1, one launch (start us, length us, event | category | flops | bytes accessed | tf_op | source)
XLA Modules:
  0.0 28.8 jit_solution(3084134760848603118)
XLA Ops:
  0.6 0.0 copy-start
  0.6 1.5 %copy.32 = s32[1,1,1,125,128]{4,3,2,1,0:T(8,128)} copy(s32[1,1,1,125,128]{4,2,3,1,0:T(1,128)} %param.16) | data formatting | bytes 128000
  2.2 1.5 %copy_bitcast_fusion.3 = (f32[125,128]{1,0:T(8,128)}, f32[125,128]{1,0:T(8,128)}) fusion(f32[1,1,1,125,128]{4,2,3,1,0:T(1,128)} %param.19, f32[1,1,1,125,128]{4,2,3,1,0:T(1,128)} %param.18), kind=kLoop, calls=%fused_computation.3 | loop fusion | bytes 256000
  3.7 1.5 %copy_bitcast_fusion.1 = (f32[125,128]{1,0:T(8,128)}, f32[125,128]{1,0:T(8,128)}) fusion(f32[1,1,1,125,128]{4,2,3,1,0:T(1,128)} %param.21, f32[1,1,1,125,128]{4,2,3,1,0:T(1,128)} %param.20), kind=kLoop, calls=%fused_computation.1 | loop fusion | bytes 256000
  5.2 0.0 copy-done
  5.2 0.9 %copy.31 = f32[1,1,1,9,125,128]{5,4,2,3,1,0:T(8,128)} copy(f32[1,1,1,9,125,128]{5,2,4,3,1,0:T(1,128)S(1)} %copy-done) | data formatting | bytes 1152000
  6.1 19.5 %shard_map.148 = (f32[3,1,9945]{2,1,0:T(1,128)}, f32[3,1,9945]{2,1,0:T(1,128)}, f32[3,1,9945]{2,1,0:T(1,128)}) custom-call(f32[3,1,9945]{2,1,0:T(1,128)} %bitcast.28, f32[3,1,9945]{2,1,0:T(1,128)} %bitcast.29, f32[3,1,9945]{2,1,0:T(1,128)} %bitcast.30, s32[125,128]{1,0:T(8,128)} %bitcast.27, f32[9,125,128]{2,1,0:T(8,128)} %bitcast.26, ...), custom_call_target="tpu_custom_call" | custom-call | tf_op jit(solution)/shard_map/pallas_call | solution.py:390
  25.6 0.0 copy-start.2
  25.6 1.6 %copy.36 = f32[3,1,1,1,9945]{4,3,2,1,0:T(1,128)} copy(f32[3,1,1,1,9945]{4,3,2,1,0:T(1,128)} %bitcast.33) | data formatting | bytes 238680
  27.2 0.0 copy-done.2
  27.2 0.0 copy-start.1
  27.2 0.6 %copy.37 = f32[3,1,1,1,9945]{4,3,2,1,0:T(1,128)} copy(f32[3,1,1,1,9945]{4,3,2,1,0:T(1,128)S(1)} %bitcast.32) | data formatting | bytes 238680
  27.9 0.3 %copy-done.1 = f32[3,1,9945]{2,1,0:T(1,128)S(1)} copy-done((f32[3,1,9945]{2,1,0:T(1,128)S(1)}, f32[3,1,9945]{2,1,0:T(1,128)}, u32[]{:S(2)}) %copy-start.1) | copy-done | bytes 119364
  28.2 0.6 %copy.38 = f32[3,1,1,1,9945]{4,3,2,1,0:T(1,128)} copy(f32[3,1,1,1,9945]{4,3,2,1,0:T(1,128)S(1)} %bitcast.31) | data formatting | bytes 238680
Async XLA Ops:
  0.6 4.6 %copy-start = (f32[1,1,1,9,125,128]{5,2,4,3,1,0:T(1,128)S(1)}, f32[1,1,1,9,125,128]{5,2,4,3,1,0:T(1,128)}, u32[]{:S(2)}) copy-start(f32[1,1,1,9,125,128]{5,2,4,3,1,0:T(1,128)} %param.17) | copy-start | bytes 1728004
  25.6 1.6 %copy-start.2 = (f32[3,1,9945]{2,1,0:T(1,128)S(1)}, f32[3,1,9945]{2,1,0:T(1,128)}, u32[]{:S(2)}) copy-start(f32[3,1,9945]{2,1,0:T(1,128)} %get-tuple-element.7) | copy-start | bytes 358024
  27.2 0.9 %copy-start.1 = (f32[3,1,9945]{2,1,0:T(1,128)S(1)}, f32[3,1,9945]{2,1,0:T(1,128)}, u32[]{:S(2)}) copy-start(f32[3,1,9945]{2,1,0:T(1,128)} %get-tuple-element.8) | copy-start | bytes 358024

commit v2 on v1

--- a/solution.py
+++ b/solution.py
@@ -90,10 +90,14 @@
     return total
 
 
+def squeezed(ref):
+    return ref.at[:, 0] if len(ref.shape) == 3 else ref.at[:, :, 0]
+
+
 def kernel(
     displ, veloc, accel, node, inv, jac, lame, shear, dens,
     select_ref, deriv_ref, back_ref, spread_ref,
-    pos_out, spd_out, acc_out,
+    acc_out,
     d_s, v_s, a_s, node_s, inv_s, jac_s, lame_s, shear_s, dens_s,
     nf, u_s, fl_s, md_s, zp_s, grid_s, acc_s,
     z_send, z_recv, y_send, y_recv, x_send, x_recv,
@@ -125,7 +129,7 @@
             )
     elems = ((node, node_s), (inv, inv_s), (jac, jac_s), (lame, lame_s), (shear, shear_s), (dens, dens_s))
     for k, (src, dst) in enumerate(elems):
-        copies.append(pltpu.make_async_copy(ELEM_SRC(src), dst, in_sem.at[9 + k]))
+        copies.append(pltpu.make_async_copy(squeezed(src), dst, in_sem.at[9 + k]))
     for cp in copies:
         cp.start()
     nf[...] = jnp.zeros_like(nf)
@@ -138,14 +142,6 @@
     half = 0.5 * time_step
     pos = d_s[...] + time_step * v_s[...] + (half * time_step) * a_s[...]
     d_s[...] = pos
-    v_s[...] = v_s[...] + half * a_s[...]
-    pos_copies = [
-        pltpu.make_async_copy(d_s.at[pl.ds(c, 1)], pos_out.at[c], out_sem.at[c])
-        for c in range(3)
-    ]
-    for cp in pos_copies:
-        cp.start()
-
     for x in range(NX):
         nf[3 * x : 3 * x + 3, 0:PLANE] = d_s[:, PLANE * x : PLANE * (x + 1)]
     planes = nf[...]
@@ -193,7 +189,7 @@
         [local[l * 128 : l * 128 + 125, c * 128 : (c + 1) * 128] for c in range(3)]
         for l in range(3)
     ]
-    maps = [[inv_s[INV_ROWS(3 * l + j)] for j in range(3)] for l in range(3)]
+    maps = [[inv_s[3 * l + j] for j in range(3)] for l in range(3)]
     weight = jac_s[...]
     lam = lame_s[...]
     mu = shear_s[...]
@@ -348,29 +344,16 @@
         force = grid_s[4 * x : 4 * x + 3, 0:PLANE]
         mass = grid_s[4 * x + 3 : 4 * x + 4, 0:PLANE]
         acc_s[:, PLANE * x : PLANE * (x + 1)] = force / mass
-    v_s[...] = v_s[...] + half * acc_s[...]
-    last = []
-    for k, (src, dst) in enumerate(((v_s, spd_out), (acc_s, acc_out))):
-        for c in range(3):
-            last.append(
-                pltpu.make_async_copy(
-                    src.at[pl.ds(c, 1)], dst.at[c], out_sem.at[3 + 3 * k + c]
-                )
-            )
+    last = [
+        pltpu.make_async_copy(acc_s.at[pl.ds(c, 1)], acc_out.at[c], out_sem.at[c])
+        for c in range(3)
+    ]
     for cp in last:
         cp.start()
     for drain in drains:
         drain()
-    for cp in pos_copies + last:
+    for cp in last:
         cp.wait()
-
-
-def ELEM_SRC(ref):
-    return ref
-
-
-def INV_ROWS(k):
-    return (k,)
 
 
 def body(displ, veloc, accel, node_index, inv_map, jac_weight, lame_first, shear_mod, density):
@@ -379,7 +362,7 @@
     select, deriv, back, spread = constants()
     fields = [x.reshape(3, 1, nodes) for x in (displ, veloc, accel)]
     elems = [
-        x.reshape(125, elements) for x in (jac_weight, lame_first, shear_mod, density)
+        x.reshape(125, 1, elements) for x in (jac_weight, lame_first, shear_mod, density)
     ]
     hbm = pl.BlockSpec(memory_space=pl.ANY)
     vmem = pl.BlockSpec(memory_space=pltpu.VMEM)
@@ -387,11 +370,11 @@
     out = jax.ShapeDtypeStruct((3, 1, nodes), f32)
     elem = pltpu.VMEM((125, elements), f32)
     width = GROUPS * SROW
-    outs = pl.pallas_call(
+    result = pl.pallas_call(
         kernel,
-        out_shape=(out, out, out),
+        out_shape=out,
         in_specs=[hbm] * 9 + [vmem] * 4,
-        out_specs=(hbm, hbm, hbm),
+        out_specs=hbm,
         scratch_shapes=[
             pltpu.VMEM((3, nodes), f32),
             pltpu.VMEM((3, nodes), f32),
@@ -413,23 +396,26 @@
             pltpu.VMEM((2, 8, WIDE), f32),
             pltpu.VMEM((2, 8, WIDE), f32),
             pltpu.SemaphoreType.DMA((15,)),
-            pltpu.SemaphoreType.DMA((9,)),
+            pltpu.SemaphoreType.DMA((3,)),
             pltpu.SemaphoreType.DMA((6,)),
             pltpu.SemaphoreType.DMA((6,)),
         ],
         compiler_params=pltpu.CompilerParams(collective_id=0, has_side_effects=True),
     )(
         *fields,
-        node_index.reshape(125, elements),
-        inv_map.reshape(9, 125, elements),
+        node_index.reshape(125, 1, elements),
+        inv_map.reshape(9, 125, 1, elements),
         *elems,
         jnp.asarray(select, jnp.bfloat16),
         jnp.asarray(deriv),
         jnp.asarray(back),
         jnp.asarray(spread),
     )
-    shape = (3, 1, 1, 1, nodes)
-    return tuple(x.reshape(shape) for x in outs)
+    half = 0.5 * time_step
+    acceleration = result.reshape(displ.shape)
+    position = displ + time_step * veloc + (half * time_step) * accel
+    speed = veloc + half * accel + half * acceleration
+    return (position, speed, acceleration)
 
 
 def solution(mesh):

time: 29.1 us -> 23.7 us (0.81)
  local copies, waits for them, and re-layouts: 8.63 us -> 0.67 us
  other arithmetic: 0 us -> 2.73 us
    unnamed x13 -> x9, local copies, waits for them, and re-layouts: 8.63 us -> 0.67 us
    unnamed x0 -> x1, other arithmetic: none -> 1.83 us
    add x0 -> x1, other arithmetic: none -> 0.9 us  [body(): position = displ + time_step * veloc + half * time_step * accel]
where the time goes in v2:
time: 23.7 us; the launch traced here: 23.5 us
  Pallas kernels  19.4 us (82%)
  other arithmetic  2.73 us (12%)
  between operations  0.68 us (3%)
  local copies, waits for them, and re-layouts  0.67 us (3%)
    pallas_call x1, Pallas kernels, body(): pl.pallas_call(kernel, out_shape=out, in_specs=[hbm] * 9 + [vmem] * 4, ou...  19.4 us
    unnamed x1, other arithmetic  1.83 us
    add x1, other arithmetic, body(): position = displ + time_step * veloc + half * time_step * accel  0.9 us
    unnamed x9, local copies, waits for them, and re-layouts  0.67 us

profile of v2, /device:TPU:1, one launch (start us, length us, event | category | flops | bytes accessed | tf_op | source)
XLA Modules:
  0.0 23.5 jit_solution(2155982077012939832)
XLA Ops:
  0.6 0.0 copy-start
  0.6 0.0 copy-start.1
  0.7 19.4 %shard_map.148 = f32[3,1,9945]{2,1,0:T(1,128)} custom-call(f32[3,1,9945]{2,1,0:T(1,128)} %bitcast.31, f32[3,1,9945]{2,1,0:T(1,128)} %bitcast.28, f32[3,1,9945]{2,1,0:T(1,128)} %bitcast.27, s32[125,1,128]{2,1,0:T(1,128)} %bitcast.32, f32[9,125,1,128]{3,2,1,0:T(1,128)} %bitcast.30, f32[125,1,128]{2,1,0:T(1,128)} %bitcast.33, f32[125,1,128]{2,1,0:T(1,128)} %bitcast.34, ...), custom_call_target="tpu_custom_call" | custom-call | tf_op jit(solution)/shard_map/pallas_call | solution.py:373
  20.1 0.0 copy-done
  20.1 0.0 copy-done.1
  20.1 0.0 copy-start.3
  20.1 1.8 %fusion.1 = f32[3,1,1,1,9945]{4,3,2,1,0:T(1,128)} fusion(f32[3,1,9945]{2,1,0:T(1,128)} %shard_map.148, f32[3,1,1,1,9945]{4,3,2,1,0:T(1,128)S(1)} %copy-done, f32[3,1,1,1,9945]{4,3,2,1,0:T(1,128)S(1)} %copy-done.1), kind=kLoop, calls=%fused_computation.2 | loop fusion | flops 119340 | bytes 477360
  21.9 0.0 copy-done.3
  21.9 0.0 copy-start.2
  21.9 0.9 %multiply_add_fusion = f32[3,1,1,1,9945]{4,3,2,1,0:T(1,128)} fusion(f32[3,1,1,1,9945]{4,3,2,1,0:T(1,128)S(1)} %copy-done, f32[3,1,1,1,9945]{4,3,2,1,0:T(1,128)S(1)} %copy-done.3, f32[3,1,1,1,9945]{4,3,2,1,0:T(1,128)S(1)} %copy-done.1), kind=kLoop, calls=%fused_computation.5 | loop fusion | flops 119340 | bytes 477360 | tf_op jit(solution)/shard_map/add | solution.py:416
  22.8 0.0 copy-done.2
  22.8 0.6 %copy.21 = f32[3,1,1,1,9945]{4,3,2,1,0:T(1,128)} copy(f32[3,1,1,1,9945]{4,3,2,1,0:T(1,128)S(1)} %bitcast.29) | data formatting | bytes 238680
Async XLA Ops:
  0.6 19.4 %copy-start = (f32[3,1,1,1,9945]{4,3,2,1,0:T(1,128)S(1)}, f32[3,1,1,1,9945]{4,3,2,1,0:T(1,128)}, u32[]{:S(2)}) copy-start(f32[3,1,1,1,9945]{4,3,2,1,0:T(1,128)} %param.15) | copy-start | bytes 358024
  0.6 19.4 %copy-start.1 = (f32[3,1,1,1,9945]{4,3,2,1,0:T(1,128)S(1)}, f32[3,1,1,1,9945]{4,3,2,1,0:T(1,128)}, u32[]{:S(2)}) copy-start(f32[3,1,1,1,9945]{4,3,2,1,0:T(1,128)} %param.14) | copy-start | bytes 358024
  20.1 1.8 %copy-start.3 = (f32[3,1,1,1,9945]{4,3,2,1,0:T(1,128)S(1)}, f32[3,1,1,1,9945]{4,3,2,1,0:T(1,128)}, u32[]{:S(2)}) copy-start(f32[3,1,1,1,9945]{4,3,2,1,0:T(1,128)} %param.13) | copy-start | bytes 358024
  21.9 0.9 %copy-start.2 = (f32[3,1,9945]{2,1,0:T(1,128)S(1)}, f32[3,1,9945]{2,1,0:T(1,128)}, u32[]{:S(2)}) copy-start(f32[3,1,9945]{2,1,0:T(1,128)} %shard_map.148) | copy-start | bytes 358024
